TPU v7x, 32 devices: a whole 2x2x4 slice. The times are simulated.
32 devices in a mesh: clip: 2 (over y), height: 4 (over z), head: 4 (over x, core).
Axes of the slice: x: 2, y: 2, z: 4, core: 2. Of those that a mesh axis runs over, the one named last changes fastest.
Arguments:
- tokens: bfloat16 [8, 192, 5120], P(('clip', 'height'), None, 'head'), parts along dimension 0, may hold values from -6 to 6
- in_sign: int32 [5120], replicated, may hold values from 0 to 1
- qkv_codes: int32 [640, 3, 3072], P(None, None, 'head'), may hold values from 0 to 65535
- qkv_scale: float32 [3, 3072], P(None, 'head'), may hold values from 0.3 to 3
- qkv_sign: int32 [3, 3072], P(None, 'head'), may hold values from 0 to 1
- windows: int32 [8, 3, 27], P(('clip', 'height')), parts along dimension 0, may hold values from 0 to 11, as said below
- oin_sign: int32 [3072], P('head'), may hold values from 0 to 1
- out_codes: int32 [384, 5120], P('head'), may hold values from 0 to 65535
- out_scale: float32 [5120], replicated, may hold values from 2 to 20
- out_sign: int32 [5120], replicated, may hold values from 0 to 1
Outputs:
- attention_out: bfloat16 [8, 192, 5120], P(('clip', 'height'), 'head'), parts along dimension 0
There are 2 independent parts, one for each index of `clip`. A program takes and returns all parts, laid end to end along the dimension named above; an argument that names none is the same for every part. Nothing has to cross between parts.
Inputs may be any that keep to these rules, and one draw needn't show every extreme that they name: `windows`: each row lists the query tile itself and 26 further entries, each one of the 27 tiles of the 3 x 3 x 3 block of tiles centred on the query tile (each of the three coordinates clipped into the grid of 1 x 4 x 3 tiles); entries may repeat and appear in any order.
All inputs are finite; a program needn't handle non-finite values.
Results may differ from a plain program's by a relative error of at most 0.015.
Values may be sent and summed in bfloat16 or wider, within the bound.
A program may use at most 128 MiB of HBM per device.

v0:
```python
import jax
import jax.numpy as jnp
import numpy as np
from jax import lax
from jax.sharding import PartitionSpec as P

D = 5120
HD = 128
HEADS = 24
HAD = 128
TILE = 64
epsilon = 1e-06


def from_behind(shard, axis, by):
    peers = lax.axis_size(axis)
    pairs = [(i, i + by) for i in range(peers) if 0 <= i + by < peers]
    return lax.ppermute(shard, axis, pairs)


def sylvester(order_size):
    matrix_now = np.ones((1, 1), np.float32)
    seed_pair = np.array([[1.0, 1.0], [1.0, -1.0]], np.float32)
    while matrix_now.shape[0] < order_size:
        matrix_now = np.kron(matrix_now, seed_pair)
    return matrix_now


def signed(sign_bits):
    return (2 * sign_bits - 1).astype(jnp.float32)


def plane_levels(packed, column_scale, fan_in):
    powers = np.array([4**k for k in range(8)], np.int32)
    powers = jnp.asarray(powers.reshape((8,) + (1,) * packed.ndim), jnp.int32)
    digits = packed[None] // powers % 4
    return ((digits.astype(jnp.float32) - 1.5) * (column_scale * fan_in ** (-0.5))).astype(
        jnp.bfloat16
    )


def plane_product(rows_in, planes):
    row_count, inner = rows_in.shape
    grouped = rows_in.reshape(row_count, inner // 8, 8)
    return jnp.einsum("nik,kic->nc", grouped, planes, preferred_element_type=jnp.float32)


def rotate_exact(matrix_in):
    row_count, columns = matrix_in.shape
    hadamard = jnp.asarray(sylvester(HAD), jnp.float32)
    grouped = matrix_in.reshape(row_count, columns // HAD, HAD)
    turned = jnp.einsum("rbi,ij->rbj", grouped, hadamard, precision=lax.Precision.HIGHEST)
    return turned.reshape(row_count, columns) * HAD ** (-0.5)


def rotate_narrow(matrix_in, sign_values):
    row_count, columns = matrix_in.shape
    flipped = matrix_in * sign_values.astype(jnp.bfloat16)
    hadamard = jnp.asarray(sylvester(HAD), jnp.bfloat16)
    grouped = flipped.reshape(row_count, columns // HAD, HAD)
    turned = jnp.einsum("rbi,ij->rbj", grouped, hadamard, preferred_element_type=jnp.float32)
    return (turned.reshape(row_count, columns) * HAD ** (-0.5)).astype(jnp.bfloat16)


def normalize(vectors):
    return vectors / jnp.sqrt(jnp.mean(vectors * vectors, axis=-1, keepdims=True) + epsilon)


def tile_allowed(listed, key_ids):
    tile_count = key_ids.shape[0]
    allowed = jnp.any(listed[:, :, None] == key_ids[None, None, :], axis=1)
    allowed = jnp.broadcast_to(allowed[:, None, :, None], (listed.shape[0], TILE, tile_count, TILE))
    return allowed.reshape(listed.shape[0] * TILE, tile_count * TILE)


def attend_block(queries, near_keys, near_values, allowed):
    score = jnp.einsum(
        "qhd,khd->hqk", queries, near_keys, preferred_element_type=jnp.float32
    ) * HD ** (-0.5)
    weight = jnp.where(allowed[None], jnp.exp(score), 0.0)
    totals = jnp.sum(weight, axis=-1)
    gathered_sum = jnp.einsum(
        "hqk,khd->qhd", weight.astype(jnp.bfloat16), near_values, preferred_element_type=jnp.float32
    )
    return (gathered_sum, totals)


def on_device(
    tokens,
    in_sign,
    qkv_codes,
    qkv_scale,
    qkv_sign,
    windows,
    oin_sign,
    out_codes,
    out_scale,
    out_sign,
):
    head_count = lax.axis_size("head")
    head_place = lax.axis_index("head")
    row_place = lax.axis_index("height")
    flat_tokens = tokens[0]
    row_count = flat_tokens.shape[0]
    qkv_planes = plane_levels(qkv_codes, qkv_scale, D)
    qkv_planes = qkv_planes.reshape(8, qkv_codes.shape[0], -1)
    whole_rows = lax.all_gather(flat_tokens, "head", axis=1, tiled=True)
    turned = rotate_narrow(whole_rows, signed(in_sign))
    projected = plane_product(turned, qkv_planes)
    local_heads = qkv_scale.shape[1] // HD
    mixed = rotate_exact(projected) * signed(qkv_sign).reshape(-1)
    mixed = mixed.reshape(row_count, 3, local_heads, HD)
    queries = normalize(mixed[:, 0]).astype(jnp.bfloat16)
    key_rows = normalize(mixed[:, 1]).astype(jnp.bfloat16)
    value_rows = mixed[:, 2].astype(jnp.bfloat16)
    key_value = jnp.stack([key_rows, value_rows])
    distances = (5, 4, 3, 1, -1, -3, -4, -5)
    neighbours = [from_behind(key_value, "height", offset) for offset in distances]
    listed = windows[0]
    qtile_count = listed.shape[0]
    tile_steps = jnp.arange(qtile_count, dtype=jnp.int32)
    own_ids = row_place * qtile_count + tile_steps
    near_ids = [(row_place - offset) * qtile_count + tile_steps for offset in distances]
    ordered = [key_value] + neighbours
    near_keys = jnp.concatenate([block[0] for block in ordered], 0)
    near_values = jnp.concatenate([block[1] for block in ordered], 0)
    all_ids = jnp.concatenate([own_ids] + near_ids, 0)
    gathered_sum, totals = attend_block(
        queries, near_keys, near_values, tile_allowed(listed, all_ids)
    )
    attended = (gathered_sum / totals.T[:, :, None]).astype(jnp.bfloat16)
    attended = attended.reshape(row_count, local_heads * HD)
    rotated_heads = rotate_narrow(attended, signed(oin_sign))
    out_planes = plane_levels(out_codes, out_scale, HEADS * HD)
    share_rows = row_count // head_count
    partial_rows = plane_product(rotated_heads, out_planes)
    summed = lax.psum(partial_rows.astype(jnp.bfloat16), "head").astype(jnp.float32)
    own_rows = lax.dynamic_slice_in_dim(summed, head_place * share_rows, share_rows, 0)
    result_rows = (rotate_exact(own_rows) * signed(out_sign)).astype(jnp.bfloat16)
    return result_rows[None]


def solution(mesh):
    return jax.shard_map(
        on_device,
        mesh=mesh,
        in_specs=(
            P(("clip", "height"), None, "head"),
            P(),
            P(None, None, "head"),
            P(None, "head"),
            P(None, "head"),
            P(("clip", "height"), None, None),
            P("head"),
            P("head", None),
            P(),
            P(),
        ),
        out_specs=P(("clip", "height"), "head", None),
        check_vma=False,
    )
```

profile of v0, /device:TPU:0, one launch (start us, length us, event | category | flops | bytes accessed | tf_op | source)
XLA Modules:
  0.0 894.5 jit_solution(4490852834834881463)
XLA Ops:
  6.5 0.7 all-gather.3.cloned.1.call-update
  7.3 0.0 all-reduce.2.cloned.1.call-start
  7.3 7.8 copy.24
  15.1 4.3 sign_compare_fusion
  19.5 490.1 %fusion.4 = bf16[18,128,640,8]{2,3,1,0:T(8,128)(2,1)} fusion(f32[18,128]{1,0:T(8,128)S(1)} %mul.173, s32[8]{0:T(128)S(1)} %copy-done.18, s32[18,128,640]{2,1,0:T(8,128)} %bitcast.138, pred[18,128,640]{2,1,0:T(8,128)(4,1)S(1)} %bitcast.142), kind=kLoop, calls=%fused_computation.8 | loop fusion | flops 247726080 | bytes 30975008 | tf_op jit(solution)/shard_map/convert_element_type | solution.py:37
  509.6 0.6 copy.39
  510.3 0.6 concatenate.10
  510.9 0.5 fusion.75
  511.4 0.6 broadcast_multiply_fusion.1
  512.0 1.3 sign_compare_fusion.1
  513.3 1.7 fusion.31
  515.0 0.3 copy.32
  515.4 0.4 copy-done.5
  515.8 2.5 multiply_convert_fusion
  518.3 3.8 copy.23
  522.1 3.4 copy.26
  525.5 15.8 %fusion.6 = f32[192,18,128,1]{2,0,3,1:T(8,128)S(1)} fusion(bf16[18,128,640,8]{2,3,1,0:T(8,128)(2,1)} %fusion.4, bf16[192,640,8]{1,0,2:T(8,128)(2,1)} %copy.26), kind=kOutput, calls=%fused_computation.11 | convolution fusion | flops 4529848320 | bytes 27328512 | tf_op jit(solution)/shard_map/nik,kic->nc/dot_general | solution.py:45
  541.3 1.6 fusion.32
  542.9 0.1 broadcast_multiply_fusion
  543.1 1.0 multiply_reduce_fusion
  544.1 0.2 fusion.51
  544.4 0.9 pad_maximum_fusion
  545.2 0.7 collective-permute-start
  546.0 0.1 compare_reduce_fusion
  546.1 0.3 broadcast_in_dim.12
  546.3 1.3 broadcast_in_dim.13
  547.7 7.3 collective-permute-start.1
  554.9 1.3 collective-permute-start.2
  556.3 1.3 collective-permute-start.3
  557.6 1.3 collective-permute-start.4
  558.9 1.0 fusion.54
  559.8 0.7 add_sqrt_fusion
  560.7 8.3 collective-permute-done.1
  569.0 11.5 %collective-permute-done.2 = bf16[2,192,6,128]{3,1,2,0:T(8,128)(2,1)S(1)} collective-permute-done((bf16[2,192,6,128]{3,1,2,0:T(8,128)(2,1)}, bf16[2,192,6,128]{3,1,2,0:T(8,128)(2,1)S(1)}, u32[]{:S(2)}, u32[]{:S(2)}) %collective-permute-start.2) | collective-permute-done | bytes 589856 | tf_op jit(solution)/shard_map/ppermute | solution.py:18
  580.5 5.3 collective-permute-done.3
  585.9 0.1 fusion.68
  586.0 5.0 fusion.17
  591.3 1.6 copy-done.7
  592.9 6.0 fusion.37
  598.9 0.2 copy.28
  599.1 237.7 %fusion.22 = bf16[192,5120]{1,0:T(8,128)(2,1)} fusion(f32[5120]{0:T(1024)} %broadcast_multiply_fusion.1, s32[8]{0:T(128)} %constant.118, s32[96,5120]{1,0:T(8,128)S(1)} %copy-done.1, pred[96,5120]{1,0:T(8,128)(4,1)S(1)} %copy-done.2, bf16[192,96,8]{0,2,1:T(8,128)(2,1)S(1)} %bitcast.144), kind=kOutput, calls=%fused_computation.30 | convolution fusion | flops 1593507840 | bytes 4739104 | tf_op jit(solution)/shard_map/nik,kic->nc/dot_general | solution.py:45
  836.8 0.0 all-reduce.2.cloned.1.call-update
  836.9 47.6 %all-reduce.2.cloned.1.call-done = bf16[192,5120]{1,0:T(8,128)(2,1)} async-done(((bf16[192,5120]{1,0:T(8,128)(2,1)}), bf16[192,5120]{1,0:T(8,128)(2,1)}) %all-reduce.2.cloned.1.call-update) | async-done | bytes 1966096 | tf_op jit(solution)/shard_map/psum | solution.py:137
  884.5 1.1 dynamic-slice_bitcast_fusion
  885.5 0.1 copy.33
  885.6 0.5 fusion.85
  886.1 0.2 reshape.147
  886.3 0.8 multiply_convert_fusion.1
  (67 shorter events, 0.8 us)
Async XLA Ops:
  6.5 506.8 %all-gather.3.cloned.1.call-start = ((), (), s32[]{:S(2)}) async-start(), calls=%async_computation.1 | async-start | bytes 2457600 | tf_op jit(solution)/shard_map/all_gather | solution.py:107
  7.3 877.2 %all-reduce.2.cloned.1.call-start = ((), (), s32[]{:S(2)}) async-start(), calls=%async_computation | async-start | bytes 3932160 | tf_op jit(solution)/shard_map/psum | solution.py:137
  15.1 4.3 copy-start.11
  15.1 4.3 copy-start.18
  19.4 490.1 %copy-start.12 = (s32[3,768]{1,0:T(4,128)S(1)}, s32[3,768]{1,0:T(4,128)}, u32[]{:S(2)}) copy-start(s32[3,768]{1,0:T(4,128)} %param.20) | copy-start | bytes 27652
  19.4 490.2 %copy-start.17 = (s32[1,3,27]{2,0,1:T(1,128)S(1)}, s32[1,3,27]{2,0,1:T(1,128)}, u32[]{:S(2)}) copy-start(s32[1,3,27]{2,0,1:T(1,128)} %param.21) | copy-start | bytes 976
  19.4 491.4 %copy-start.14 = (s32[768]{0:T(1024)S(1)}, s32[768]{0:T(1024)}, u32[]{:S(2)}) copy-start(s32[768]{0:T(1024)} %param.22) | copy-start | bytes 9220
  19.5 492.0 %copy-start.10 = (s32[5120]{0:T(1024)S(1)}, s32[5120]{0:T(1024)}, u32[]{:S(2)}) copy-start(s32[5120]{0:T(1024)} %param.17) | copy-start | bytes 61444
  19.5 492.0 %copy-start.8 = (f32[5120]{0:T(1024)S(1)}, f32[5120]{0:T(1024)}, u32[]{:S(2)}) copy-start(f32[5120]{0:T(1024)} %param.24) | copy-start | bytes 61444
  19.5 492.6 %copy-start = (s32[96,5120]{1,0:T(8,128)S(1)}, s32[96,5120]{1,0:T(8,128)}, u32[]{:S(2)}) copy-start(s32[96,5120]{1,0:T(8,128)} %param.23) | copy-start | bytes 5898244
  515.0 0.8 copy-start.5
  525.5 15.8 %copy-start.3 = (f32[128,128,1]{1,0,2:T(8,128)S(1)}, f32[128,128,1]{1,0,2:T(8,128)}, u32[]{:S(2)}) copy-start(f32[128,128,1]{1,0,2:T(8,128)} %constant.125) | copy-start | bytes 196612
  543.1 2.9 copy-start.13
  543.1 2.9 copy-start.16
  544.1 1.8 copy-start.4
  545.2 15.3 %collective-permute-start = (bf16[2,192,6,128]{3,1,2,0:T(8,128)(2,1)}, bf16[2,192,6,128]{3,1,2,0:T(8,128)(2,1)S(1)}, u32[]{:S(2)}, u32[]{:S(2)}) collective-permute-start(bf16[2,192,6,128]{3,1,2,0:T(8,128)(2,1)} %pad_maximum_fusion), channel_id=1, source_target_pairs={} | collective-permute-start | bytes 1769480 | tf_op jit(solution)/shard_map/ppermute | solution.py:18
  547.7 21.3 %collective-permute-start.1 = (bf16[2,192,6,128]{3,1,2,0:T(8,128)(2,1)}, bf16[2,192,6,128]{3,1,2,0:T(8,128)(2,1)S(1)}, u32[]{:S(2)}, u32[]{:S(2)}) collective-permute-start(bf16[2,192,6,128]{3,1,2,0:T(8,128)(2,1)} %pad_maximum_fusion), channel_id=1, source_target_pairs={{0,12},{1,13},{2,14},{3,15},{16,28},{17,29},{18,30},{19,31}} | collective-permute-start | bytes 1769480 | tf_op jit(solution)/shard_map/ppermute | solution.py:18
  554.9 25.5 %collective-permute-start.2 = (bf16[2,192,6,128]{3,1,2,0:T(8,128)(2,1)}, bf16[2,192,6,128]{3,1,2,0:T(8,128)(2,1)S(1)}, u32[]{:S(2)}, u32[]{:S(2)}) collective-permute-start(bf16[2,192,6,128]{3,1,2,0:T(8,128)(2,1)} %pad_maximum_fusion), channel_id=1, source_target_pairs={{0,4},{4,8},{8,12},{1,5},{5,9},{9,13},{2,6},{6,10},{10,14},{3,7},{... | collective-permute-start | bytes 1769480 | tf_op jit(solution)/shard_map/ppermute | solution.py:18
  556.3 29.5 %collective-permute-start.3 = (bf16[2,192,6,128]{3,1,2,0:T(8,128)(2,1)}, bf16[2,192,6,128]{3,1,2,0:T(8,128)(2,1)S(1)}, u32[]{:S(2)}, u32[]{:S(2)}) collective-permute-start(bf16[2,192,6,128]{3,1,2,0:T(8,128)(2,1)} %pad_maximum_fusion), channel_id=1, source_target_pairs={{4,0},{8,4},{12,8},{5,1},{9,5},{13,9},{6,2},{10,6},{14,10},{7,3},{... | collective-permute-start | bytes 1769480 | tf_op jit(solution)/shard_map/ppermute | solution.py:18
  557.6 28.2 %collective-permute-start.4 = (bf16[2,192,6,128]{3,1,2,0:T(8,128)(2,1)}, bf16[2,192,6,128]{3,1,2,0:T(8,128)(2,1)S(1)}, u32[]{:S(2)}, u32[]{:S(2)}) collective-permute-start(bf16[2,192,6,128]{3,1,2,0:T(8,128)(2,1)} %pad_maximum_fusion), channel_id=1, source_target_pairs={{12,0},{13,1},{14,2},{15,3},{28,16},{29,17},{30,18},{31,19}} | collective-permute-start | bytes 1769480 | tf_op jit(solution)/shard_map/ppermute | solution.py:18
  591.0 1.9 copy-start.6
  591.0 1.9 copy-start.15
  591.3 1.6 copy-start.7
  592.9 6.2 copy-start.1
  592.9 6.2 copy-start.2
  599.1 237.7 %copy-start.9 = (s32[5120]{0:T(1024)S(1)}, s32[5120]{0:T(1024)}, u32[]{:S(2)}) copy-start(s32[5120]{0:T(1024)} %param.25) | copy-start | bytes 61444
Sparse Core Ops, SparseCore 0:
  8.9 24.5 all-gather.2
  837.0 47.4 all-reduce.1
where the time goes:
time: 908 us; the launch traced here: 894 us
  other arithmetic  503 us (55%)
  matrix products  269 us (30%)
  waiting for transfers between devices  73.3 us (8%)
  local copies, waits for them, and re-layouts  22.3 us (2%)
  between operations  14.5 us (2%)
  starting transfers between devices  11.9 us (1%)
    convert_element_type x1, other arithmetic, plane_levels(): ((digits.astype(jnp.float32) - 1.5) * (column_scale * fan_in ** (-0.5)))....  490 us
    dot_general x2, matrix products, plane_product(): jnp.einsum('nik,kic->nc', grouped, planes, preferred_element_type=jnp.flo...  253 us
    psum x1, waiting for transfers between devices, on_device(): lax.psum(partial_rows.astype(jnp.bfloat16), 'head').astype(jnp.float32)  47.6 us
    ppermute x5, waiting for transfers between devices, from_behind(): return lax.ppermute(shard, axis, pairs)  25 us
  transfers between devices with their start and end apart: 7, of which 4 were waited for; matrix products, arithmetic and copies ran while one was open for 57% of the time, Pallas kernels for 0%

commit v1 on v0

--- a/solution.py
+++ b/solution.py
@@ -10,6 +10,12 @@
 HAD = 128
 TILE = 64
 epsilon = 1e-06
+
+
+def summed_here(x, axis):
+    shards = lax.all_gather(x, axis, axis=0, tiled=False)
+    total = shards.sum(axis=0)
+    return total
 
 
 def from_behind(shard, axis, by):
@@ -134,7 +140,7 @@
     out_planes = plane_levels(out_codes, out_scale, HEADS * HD)
     share_rows = row_count // head_count
     partial_rows = plane_product(rotated_heads, out_planes)
-    summed = lax.psum(partial_rows.astype(jnp.bfloat16), "head").astype(jnp.float32)
+    summed = summed_here(partial_rows.astype(jnp.bfloat16), "head").astype(jnp.float32)
     own_rows = lax.dynamic_slice_in_dim(summed, head_place * share_rows, share_rows, 0)
     result_rows = (rotate_exact(own_rows) * signed(out_sign)).astype(jnp.bfloat16)
     return result_rows[None]

time: 908 us -> 918 us (1.011)
    all_gather x0 -> x1, waiting for transfers between devices: none -> 53.6 us  [summed_here(): shards = lax.all_gather(x, axis, axis=0, tiled=False)]
    psum x1 -> x0, waiting for transfers between devices: 47.6 us -> none  [on_device(): lax.psum(partial_rows.astype(jnp.bfloat16), 'head').astype(jnp.float32)]
  transfers between devices with their start and end apart: 7 -> 7, of which waited for: 4 -> 4; matrix products, arithmetic and copies ran while one was open for 57% -> 56% of each run, Pallas kernels for 0% -> 0%
where the time goes in v1:
time: 918 us; the launch traced here: 905 us
  other arithmetic  508 us (55%)
  matrix products  270 us (29%)
  waiting for transfers between devices  79.4 us (9%)
  local copies, waits for them, and re-layouts  21.3 us (2%)
  between operations  14.5 us (2%)
  starting transfers between devices  11.9 us (1%)
    convert_element_type x1, other arithmetic, plane_levels(): ((digits.astype(jnp.float32) - 1.5) * (column_scale * fan_in ** (-0.5)))....  490 us
    dot_general x2, matrix products, plane_product(): jnp.einsum('nik,kic->nc', grouped, planes, preferred_element_type=jnp.flo...  255 us
    all_gather x1, waiting for transfers between devices, summed_here(): shards = lax.all_gather(x, axis, axis=0, tiled=False)  53.6 us
    ppermute x5, waiting for transfers between devices, from_behind(): return lax.ppermute(shard, axis, pairs)  25 us
  transfers between devices with their start and end apart: 7, of which 4 were waited for; matrix products, arithmetic and copies ran while one was open for 56% of the time, Pallas kernels for 0%

profile of v1, /device:TPU:0, one launch (start us, length us, event | category | flops | bytes accessed | tf_op | source)
XLA Modules:
  0.0 905.5 jit_solution(16786760657270790944)
XLA Ops:
  6.5 0.7 all-gather.5.cloned.1.call-update
  7.3 0.0 all-gather.7.cloned.1.call-start
  7.3 7.8 copy.24
  15.1 4.3 sign_compare_fusion
  19.5 490.1 %fusion.4 = bf16[18,128,640,8]{2,3,1,0:T(8,128)(2,1)} fusion(f32[18,128]{1,0:T(8,128)S(1)} %mul.173, s32[8]{0:T(128)S(1)} %copy-done.18, s32[18,128,640]{2,1,0:T(8,128)} %bitcast.139, pred[18,128,640]{2,1,0:T(8,128)(4,1)S(1)} %bitcast.144), kind=kLoop, calls=%fused_computation.8 | loop fusion | flops 247726080 | bytes 30975008 | tf_op jit(solution)/shard_map/convert_element_type | solution.py:43
  509.6 0.6 copy.39
  510.3 0.6 concatenate.10
  510.9 0.5 fusion.75
  511.4 0.6 broadcast_multiply_fusion.1
  512.0 1.3 sign_compare_fusion.1
  513.3 1.7 fusion.31
  515.0 0.3 copy.32
  515.4 0.4 copy-done.5
  515.8 2.5 multiply_convert_fusion
  518.3 3.8 copy.23
  522.1 3.4 copy.26
  525.5 15.8 %fusion.6 = f32[192,18,128,1]{2,0,3,1:T(8,128)S(1)} fusion(bf16[18,128,640,8]{2,3,1,0:T(8,128)(2,1)} %fusion.4, bf16[192,640,8]{1,0,2:T(8,128)(2,1)} %copy.26), kind=kOutput, calls=%fused_computation.11 | convolution fusion | flops 4529848320 | bytes 27328512 | tf_op jit(solution)/shard_map/nik,kic->nc/dot_general | solution.py:51
  541.3 1.6 fusion.32
  542.9 0.1 broadcast_multiply_fusion
  543.1 1.0 multiply_reduce_fusion
  544.1 0.2 fusion.51
  544.4 0.9 pad_maximum_fusion
  545.2 0.7 collective-permute-start
  546.0 0.1 compare_reduce_fusion
  546.1 0.3 broadcast_in_dim.12
  546.3 1.3 broadcast_in_dim.13
  547.7 7.3 collective-permute-start.1
  554.9 1.3 collective-permute-start.2
  556.3 1.3 collective-permute-start.3
  557.6 1.3 collective-permute-start.4
  558.9 1.0 fusion.54
  559.8 0.7 add_sqrt_fusion
  560.7 8.3 collective-permute-done.1
  569.0 11.5 %collective-permute-done.2 = bf16[2,192,6,128]{3,1,2,0:T(8,128)(2,1)S(1)} collective-permute-done((bf16[2,192,6,128]{3,1,2,0:T(8,128)(2,1)}, bf16[2,192,6,128]{3,1,2,0:T(8,128)(2,1)S(1)}, u32[]{:S(2)}, u32[]{:S(2)}) %collective-permute-start.2) | collective-permute-done | bytes 589856 | tf_op jit(solution)/shard_map/ppermute | solution.py:24
  580.5 5.3 collective-permute-done.3
  585.9 0.1 fusion.68
  586.0 5.0 fusion.17
  591.3 1.6 copy-done.7
  592.9 6.0 fusion.37
  598.9 0.2 copy.28
  599.1 238.8 %fusion.22 = bf16[192,5120]{1,0:T(8,128)(2,1)} fusion(f32[5120]{0:T(1024)} %broadcast_multiply_fusion.1, s32[8]{0:T(128)} %constant.120, s32[96,5120]{1,0:T(8,128)S(1)} %copy-done.1, pred[96,5120]{1,0:T(8,128)(4,1)S(1)} %copy-done.2, bf16[192,96,8]{0,2,1:T(8,128)(2,1)S(1)} %bitcast.146), kind=kOutput, calls=%fused_computation.30 | convolution fusion | flops 1593507840 | bytes 4739104 | tf_op jit(solution)/shard_map/nik,kic->nc/dot_general | solution.py:51
  837.9 0.0 all-gather.7.cloned.1.call-update
  838.0 53.6 %all-gather.7.cloned.1.call-done = bf16[768,5120]{1,0:T(8,128)(2,1)} async-done(((bf16[192,5120]{1,0:T(8,128)(2,1)}), bf16[768,5120]{1,0:T(8,128)(2,1)}) %all-gather.7.cloned.1.call-update) | async-done | bytes 7864336 | tf_op jit(solution)/shard_map/all_gather | solution.py:16
  891.6 4.8 reduce_sum.42
  896.5 0.1 copy.33
  896.6 0.5 fusion.85
  897.1 0.2 reshape.147
  897.3 0.8 multiply_convert_fusion.1
  (68 shorter events, 0.8 us)
Async XLA Ops:
  6.5 506.8 %all-gather.5.cloned.1.call-start = ((), (), s32[]{:S(2)}) async-start(), calls=%async_computation | async-start | bytes 2457600 | tf_op jit(solution)/shard_map/all_gather | solution.py:113
  7.3 884.3 %all-gather.7.cloned.1.call-start = ((), (), s32[]{:S(2)}) async-start(), calls=%async_computation.1 | async-start | bytes 9830400 | tf_op jit(solution)/shard_map/all_gather | solution.py:16
  15.1 4.3 copy-start.11
  15.1 4.3 copy-start.18
  19.4 490.1 %copy-start.12 = (s32[3,768]{1,0:T(4,128)S(1)}, s32[3,768]{1,0:T(4,128)}, u32[]{:S(2)}) copy-start(s32[3,768]{1,0:T(4,128)} %param.20) | copy-start | bytes 27652
  19.4 490.2 %copy-start.17 = (s32[1,3,27]{2,0,1:T(1,128)S(1)}, s32[1,3,27]{2,0,1:T(1,128)}, u32[]{:S(2)}) copy-start(s32[1,3,27]{2,0,1:T(1,128)} %param.21) | copy-start | bytes 976
  19.4 491.4 %copy-start.14 = (s32[768]{0:T(1024)S(1)}, s32[768]{0:T(1024)}, u32[]{:S(2)}) copy-start(s32[768]{0:T(1024)} %param.22) | copy-start | bytes 9220
  19.5 492.0 %copy-start.10 = (s32[5120]{0:T(1024)S(1)}, s32[5120]{0:T(1024)}, u32[]{:S(2)}) copy-start(s32[5120]{0:T(1024)} %param.17) | copy-start | bytes 61444
  19.5 492.0 %copy-start.8 = (f32[5120]{0:T(1024)S(1)}, f32[5120]{0:T(1024)}, u32[]{:S(2)}) copy-start(f32[5120]{0:T(1024)} %param.24) | copy-start | bytes 61444
  19.5 492.6 %copy-start = (s32[96,5120]{1,0:T(8,128)S(1)}, s32[96,5120]{1,0:T(8,128)}, u32[]{:S(2)}) copy-start(s32[96,5120]{1,0:T(8,128)} %param.23) | copy-start | bytes 5898244
  515.0 0.8 copy-start.5
  525.5 15.8 %copy-start.3 = (f32[128,128,1]{1,0,2:T(8,128)S(1)}, f32[128,128,1]{1,0,2:T(8,128)}, u32[]{:S(2)}) copy-start(f32[128,128,1]{1,0,2:T(8,128)} %constant.127) | copy-start | bytes 196612
  543.1 2.9 copy-start.13
  543.1 2.9 copy-start.16
  544.1 1.8 copy-start.4
  545.2 15.3 %collective-permute-start = (bf16[2,192,6,128]{3,1,2,0:T(8,128)(2,1)}, bf16[2,192,6,128]{3,1,2,0:T(8,128)(2,1)S(1)}, u32[]{:S(2)}, u32[]{:S(2)}) collective-permute-start(bf16[2,192,6,128]{3,1,2,0:T(8,128)(2,1)} %pad_maximum_fusion), channel_id=1, source_target_pairs={} | collective-permute-start | bytes 1769480 | tf_op jit(solution)/shard_map/ppermute | solution.py:24
  547.7 21.3 %collective-permute-start.1 = (bf16[2,192,6,128]{3,1,2,0:T(8,128)(2,1)}, bf16[2,192,6,128]{3,1,2,0:T(8,128)(2,1)S(1)}, u32[]{:S(2)}, u32[]{:S(2)}) collective-permute-start(bf16[2,192,6,128]{3,1,2,0:T(8,128)(2,1)} %pad_maximum_fusion), channel_id=1, source_target_pairs={{0,12},{1,13},{2,14},{3,15},{16,28},{17,29},{18,30},{19,31}} | collective-permute-start | bytes 1769480 | tf_op jit(solution)/shard_map/ppermute | solution.py:24
  554.9 25.5 %collective-permute-start.2 = (bf16[2,192,6,128]{3,1,2,0:T(8,128)(2,1)}, bf16[2,192,6,128]{3,1,2,0:T(8,128)(2,1)S(1)}, u32[]{:S(2)}, u32[]{:S(2)}) collective-permute-start(bf16[2,192,6,128]{3,1,2,0:T(8,128)(2,1)} %pad_maximum_fusion), channel_id=1, source_target_pairs={{0,4},{4,8},{8,12},{1,5},{5,9},{9,13},{2,6},{6,10},{10,14},{3,7},{... | collective-permute-start | bytes 1769480 | tf_op jit(solution)/shard_map/ppermute | solution.py:24
  556.3 29.5 %collective-permute-start.3 = (bf16[2,192,6,128]{3,1,2,0:T(8,128)(2,1)}, bf16[2,192,6,128]{3,1,2,0:T(8,128)(2,1)S(1)}, u32[]{:S(2)}, u32[]{:S(2)}) collective-permute-start(bf16[2,192,6,128]{3,1,2,0:T(8,128)(2,1)} %pad_maximum_fusion), channel_id=1, source_target_pairs={{4,0},{8,4},{12,8},{5,1},{9,5},{13,9},{6,2},{10,6},{14,10},{7,3},{... | collective-permute-start | bytes 1769480 | tf_op jit(solution)/shard_map/ppermute | solution.py:24
  557.6 28.2 %collective-permute-start.4 = (bf16[2,192,6,128]{3,1,2,0:T(8,128)(2,1)}, bf16[2,192,6,128]{3,1,2,0:T(8,128)(2,1)S(1)}, u32[]{:S(2)}, u32[]{:S(2)}) collective-permute-start(bf16[2,192,6,128]{3,1,2,0:T(8,128)(2,1)} %pad_maximum_fusion), channel_id=1, source_target_pairs={{12,0},{13,1},{14,2},{15,3},{28,16},{29,17},{30,18},{31,19}} | collective-permute-start | bytes 1769480 | tf_op jit(solution)/shard_map/ppermute | solution.py:24
  591.0 1.9 copy-start.6
  591.0 1.9 copy-start.15
  591.3 1.6 copy-start.7
  592.9 6.2 copy-start.1
  592.9 6.2 copy-start.2
  599.1 238.8 %copy-start.9 = (s32[5120]{0:T(1024)S(1)}, s32[5120]{0:T(1024)}, u32[]{:S(2)}) copy-start(s32[5120]{0:T(1024)} %param.25) | copy-start | bytes 61444
Sparse Core Ops, SparseCore 0:
  8.9 24.5 all-gather.4
  838.0 53.5 all-gather.6
